TPU v7x, 32 devices: a whole 2x2x4 slice. The times are simulated.
32 devices in a mesh: dp: 4 (over x, core), expert: 8 (over z, y).
Axes of the slice: x: 2, y: 2, z: 4, core: 2. Of those that a mesh axis runs over, the one named last changes fastest.
Arguments:
- tokens: bfloat16 [4096, 2048], P(('dp', 'expert')), may hold values from -6 to 6
- expert_ids: int32 [4096, 8], P(('dp', 'expert')), may hold values from 0 to 127, all different within a row; in each aligned block of 128 rows (0 to 127, 128 to 255, ...) at most 20 rows name the same one
- gate_probs: float32 [4096, 8], P(('dp', 'expert')), may hold values from 0.05 to 1
- gate_weight: bfloat16 [128, 768, 2048], P(('dp', 'expert')), may hold values from -0.125 to 0.125
- up_weight: bfloat16 [128, 768, 2048], P(('dp', 'expert')), may hold values from -0.125 to 0.125
- down_weight: bfloat16 [128, 768, 2048], P(('dp', 'expert')), may hold values from -0.4375 to 0.4375
Outputs:
- mixed: bfloat16 [4096, 2048], P(('dp', 'expert'))
- expert_load: float32 [128], replicated
Inputs may be any that keep to these rules, and one draw needn't show every extreme that they name: `expert_ids`: in each block of 128 consecutive tokens no expert is named by more than 20 pairs, a bound that some blocks reach; every expert is named somewhere.
All inputs are finite; a program needn't handle non-finite values.
Results may differ from a plain program's by a relative error of at most 0.0085.
Values may be sent and summed in bfloat16 or wider, within the bound.
A program may use at most 128 MiB of HBM per device.

v0:
```python
import jax
import jax.numpy as jnp
from jax import lax
from jax.sharding import PartitionSpec as P

CAP = 20


def expert_block(arrived, gate_weight, up_weight, down_weight):
    gate_part = jnp.einsum(
        "sekd,efd->sekf", arrived, gate_weight, preferred_element_type=jnp.float32
    )
    up_part = jnp.einsum("sekd,efd->sekf", arrived, up_weight, preferred_element_type=jnp.float32)
    hidden = (jax.nn.silu(gate_part) * up_part).astype(jnp.bfloat16)
    produced = jnp.einsum("sekf,efd->sekd", hidden, down_weight, preferred_element_type=jnp.float32)
    return produced.astype(jnp.bfloat16)


def on_device(tokens, expert_ids, gate_probs, gate_weight, up_weight, down_weight):
    tok_rows, features = tokens.shape
    chosen = expert_ids.shape[1]
    owned = gate_weight.shape[0]
    devices = lax.axis_size(("dp", "expert"))
    experts = owned * devices
    pairs = tok_rows * chosen
    flat_ids = expert_ids.reshape(pairs)
    one_hot = (flat_ids[:, None] == lax.iota(jnp.int32, experts)[None, :]).astype(jnp.int32)
    earlier = jnp.cumsum(one_hot, axis=0) - one_hot
    slot_index = jnp.sum(earlier * one_hot, axis=1)
    target = flat_ids * CAP + slot_index
    owner_row = lax.iota(jnp.int32, pairs) // chosen
    source_row = jnp.full((experts * CAP,), tok_rows, jnp.int32).at[target].set(owner_row)
    padded = jnp.concatenate([tokens, jnp.zeros((1, features), tokens.dtype)], axis=0)
    outgoing = padded[source_row].reshape(devices, owned, CAP, features)
    counts = lax.psum(jnp.sum(one_hot, axis=0).astype(jnp.float32), ("dp", "expert"))
    produced = expert_block(
        lax.all_to_all(outgoing, ("dp", "expert"), split_axis=0, concat_axis=0, tiled=True),
        gate_weight,
        up_weight,
        down_weight,
    )
    returned = lax.all_to_all(produced, ("dp", "expert"), split_axis=0, concat_axis=0, tiled=True)
    results = returned.reshape(experts * CAP, features)
    picked = results[target].reshape(tok_rows, chosen, features)
    weights = gate_probs / jnp.sum(gate_probs, axis=1, keepdims=True)
    mixed = jnp.einsum("tk,tkd->td", weights, picked.astype(jnp.float32)).astype(jnp.bfloat16)
    expert_load = counts * (experts / (tok_rows * devices * chosen))
    return (mixed, expert_load)


def solution(mesh):
    in_specs = (
        P(("dp", "expert"), None),
        P(("dp", "expert"), None),
        P(("dp", "expert"), None),
        P(("dp", "expert"), None, None),
        P(("dp", "expert"), None, None),
        P(("dp", "expert"), None, None),
    )
    out_specs = (P(("dp", "expert"), None), P())
    return jax.shard_map(
        on_device, mesh=mesh, in_specs=in_specs, out_specs=out_specs, check_vma=False
    )
```

profile of v0, /device:TPU:0, one launch (start us, length us, event | category | flops | bytes accessed | tf_op | source)
XLA Modules:
  0.0 692.8 jit_solution(644135197542510640)
XLA Ops:
  0.6 0.8 copy.24
  1.4 0.1 eq.29
  1.5 0.1 eq.25
  1.6 0.7 broadcast_multiply_fusion
  2.3 0.1 copy.26
  2.4 0.2 fusion.22
  2.7 0.1 copy.27
  2.8 0.1 copy.23
  2.9 0.1 mul.34
  3.0 0.4 convert_reduce_fusion
  3.4 4.3 scatter_custom_fusion
  7.7 1.1 concatenate.3
  8.8 10.9 %gather_fusion = bf16[2560,2048]{1,0:T(8,128)(2,1)} fusion(bf16[129,2048]{1,0:T(8,128)(2,1)S(1)} %concatenate.3, s32[3072]{0:T(1024)S(1)} %pad_clamp_fusion), kind=kCustom, calls=%fused_computation | custom fusion | bytes 20981760 | tf_op jit(solution)/shard_map/gather | solution.py:34
  19.7 16.4 %reshape.61 = bf16[32,4,20,2048]{3,2,1,0:T(8,128)(2,1)} reshape(bf16[2560,2048]{1,0:T(8,128)(2,1)} %gather_fusion) | data formatting | bytes 20971520 | tf_op jit(solution)/shard_map/reshape | solution.py:34
  36.1 12.8 %copy.28 = bf16[32,4,20,2048]{3,1,2,0:T(4,128)(2,1)S(1)} copy(bf16[32,4,20,2048]{3,2,1,0:T(8,128)(2,1)} %reshape.61) | data formatting | bytes 20971520 | tf_op jit(solution)/shard_map/reshape | solution.py:34
  48.9 237.2 %all_to_all.10 = bf16[32,4,20,2048]{3,1,2,0:T(4,128)(2,1)} all-to-all(bf16[32,4,20,2048]{3,1,2,0:T(4,128)(2,1)S(1)} %copy.28), channel_id=1, replica_groups=mesh['dp'=4,'expert'=8] {'dp','expert'}, dimensions={0} | all-to-all | bytes 20971520 | tf_op jit(solution)/shard_map/all_to_all | solution.py:37
  286.1 27.1 %fusion.2 = f32[4,32,20,768]{3,1,2,0:T(8,128)} fusion(bf16[4,768,2048]{2,1,0:T(8,128)(2,1)} %param.10, bf16[32,4,20,2048]{3,1,2,0:T(4,128)(2,1)} %all_to_all.10), kind=kOutput, calls=%fused_computation.5 | convolution fusion | flops 8053063680 | bytes 30932992 | tf_op jit(solution)/shard_map/sekd,efd->sekf/dot_general | solution.py:13
  313.2 32.7 %fusion.8 = bf16[32,4,20,768]{3,0,2,1:T(8,128)(2,1)} fusion(f32[4,32,20,768]{3,1,2,0:T(8,128)} %fusion.2, bf16[4,768,2048]{2,1,0:T(8,128)(2,1)} %param.9, bf16[32,4,20,2048]{3,1,2,0:T(4,128)(2,1)} %all_to_all.10), kind=kOutput, calls=%fused_computation.13 | convolution fusion | flops 8064860160 | bytes 34865152 | tf_op jit(solution)/shard_map/sekd,efd->sekf/dot_general | solution.py:10
  345.9 14.2 %convert_bitcast_fusion = bf16[32,4,20,2048]{3,0,2,1:T(8,128)(2,1)S(1)} fusion(bf16[32,4,20,768]{3,0,2,1:T(8,128)(2,1)} %fusion.8, bf16[4,768,2048]{2,1,0:T(8,128)(2,1)} %param.11), kind=kOutput, calls=%fused_computation.9 | convolution fusion | flops 8058306560 | bytes 27000832 | tf_op jit(solution)/shard_map/sekf,efd->sekd/dot_general | solution.py:15
  360.2 24.1 %copy.31 = bf16[32,4,20,2048]{3,1,2,0:T(4,128)(2,1)} copy(bf16[32,4,20,2048]{3,0,2,1:T(8,128)(2,1)S(1)} %convert_bitcast_fusion) | data formatting | bytes 20971520 | tf_op jit(solution)/shard_map/convert_element_type | solution.py:16
  384.3 0.0 copy-start
  384.3 3.9 all-to-all-start.1
  388.1 0.0 copy-done
  388.2 0.1 copy.36
  388.3 254.7 %psum.7 = f32[128]{0:T(128)S(1)} all-reduce(f32[128]{0:T(128)S(1)} %convert_element_type.29), channel_id=1, replica_groups=mesh['dp'=4,'expert'=8] {'dp','expert'}, use_global_device_ids=true, to_apply=%region_6.7 | all-reduce | flops 128 | bytes 1024 | tf_op jit(solution)/shard_map/psum | solution.py:35
  643.0 0.5 broadcast_multiply_fusion.1
  643.5 0.0 all-to-all-done.1
  643.5 14.0 %copy.32 = bf16[32,4,20,2048]{3,2,1,0:T(8,128)(2,1)} copy(bf16[32,4,20,2048]{3,1,2,0:T(4,128)(2,1)} %all-to-all-done.1) | data formatting | bytes 20971520 | tf_op jit(solution)/shard_map/all_to_all | solution.py:42
  657.5 16.5 %reshape.62 = bf16[2560,2048]{1,0:T(8,128)(2,1)} reshape(bf16[32,4,20,2048]{3,2,1,0:T(8,128)(2,1)} %copy.32) | data formatting | bytes 20971520 | tf_op jit(solution)/shard_map/reshape | solution.py:43
  674.0 14.2 %gather_fusion.1 = bf16[1024,2048]{1,0:T(8,128)(2,1)} fusion(bf16[2560,2048]{1,0:T(8,128)(2,1)} %reshape.62, s32[1024]{0:T(1024)S(1)} %broadcast_clamp_fusion), kind=kCustom, calls=%fused_computation.1 | custom fusion | bytes 8392704 | tf_op jit(solution)/shard_map/gather | solution.py:44
  688.1 3.4 fusion.18
  691.6 1.1 copy.45
  (12 shorter events, 0.1 us)
Async XLA Ops:
  384.3 3.9 copy-start
  384.3 259.3 %all-to-all-start.1 = ((bf16[32,4,20,2048]{3,1,2,0:T(4,128)(2,1)}), bf16[32,4,20,2048]{3,1,2,0:T(4,128)(2,1)}, u32[]{:S(2)}, u32[]{:S(2)}) async-start(bf16[32,4,20,2048]{3,1,2,0:T(4,128)(2,1)} %copy.31), calls=%async_computation.1 | async-start | bytes 20971520 | tf_op jit(solution)/shard_map/all_to_all | solution.py:42
where the time goes:
time: 698 us; the launch traced here: 693 us
  blocking collectives  492 us (70%)
  local copies, waits for them, and re-layouts  117 us (17%)
  matrix products  77.5 us (11%)
    psum x1, blocking collectives, on_device(): lax.psum(jnp.sum(one_hot, axis=0).astype(jnp.float32), ('dp', 'expert'))  255 us
    all_to_all x1, blocking collectives, on_device(): lax.all_to_all(outgoing, ('dp', 'expert'), split_axis=0, concat_axis=0, t...  237 us
    dot_general x1, matrix products, expert_block(): jnp.einsum('sekd,efd->sekf', arrived, gate_weight, preferred_element_type...  32.7 us
    reshape x2, local copies, waits for them, and re-layouts, on_device(): outgoing = padded[source_row].reshape(devices, owned, CAP, features)  29.1 us
    dot_general x1, matrix products, expert_block(): jnp.einsum('sekd,efd->sekf', arrived, up_weight, preferred_element_type=j...  27.1 us
    convert_element_type x1, local copies, waits for them, and re-layouts, expert_block(): return produced.astype(jnp.bfloat16)  24.1 us
    reshape x1, local copies, waits for them, and re-layouts, on_device(): results = returned.reshape(experts * CAP, features)  16.5 us
    dot_general x1, matrix products, expert_block(): jnp.einsum('sekf,efd->sekd', hidden, down_weight, preferred_element_type=...  14.2 us
  transfers between devices with their start and end apart: 1, of which 0 were waited for; matrix products, arithmetic and copies ran while one was open for 0% of the time, Pallas kernels for 0%

commit v1 on v0

--- a/solution.py
+++ b/solution.py
@@ -32,7 +32,12 @@
     source_row = jnp.full((experts * CAP,), tok_rows, jnp.int32).at[target].set(owner_row)
     padded = jnp.concatenate([tokens, jnp.zeros((1, features), tokens.dtype)], axis=0)
     outgoing = padded[source_row].reshape(devices, owned, CAP, features)
-    counts = lax.psum(jnp.sum(one_hot, axis=0).astype(jnp.float32), ("dp", "expert"))
+
+    def pair_matrix(own_rows, shard_axis):
+        f_now = lax.all_gather(own_rows, axis_name=shard_axis)
+        return jnp.sum(f_now, axis=0)
+
+    counts = pair_matrix(jnp.sum(one_hot, axis=0).astype(jnp.float32), ("dp", "expert"))
     produced = expert_block(
         lax.all_to_all(outgoing, ("dp", "expert"), split_axis=0, concat_axis=0, tiled=True),
         gate_weight,

time: 698 us -> 723 us (1.036)
  blocking collectives: 492 us -> 521 us
    all_gather x0 -> x1, blocking collectives: none -> 284 us  [pair_matrix(): f_now = lax.all_gather(own_rows, axis_name=shard_axis)]
    psum x1 -> x0, blocking collectives: 255 us -> none  [on_device(): lax.psum(jnp.sum(one_hot, axis=0).astype(jnp.float32), ('dp', 'expert'))]
where the time goes in v1:
time: 723 us; the launch traced here: 721 us
  blocking collectives  521 us (72%)
  local copies, waits for them, and re-layouts  117 us (16%)
  matrix products  76.7 us (11%)
    all_gather x1, blocking collectives, pair_matrix(): f_now = lax.all_gather(own_rows, axis_name=shard_axis)  284 us
    all_to_all x1, blocking collectives, on_device(): lax.all_to_all(outgoing, ('dp', 'expert'), split_axis=0, concat_axis=0, t...  237 us
    dot_general x1, matrix products, expert_block(): jnp.einsum('sekd,efd->sekf', arrived, gate_weight, preferred_element_type...  32.5 us
    reshape x2, local copies, waits for them, and re-layouts, on_device(): outgoing = padded[source_row].reshape(devices, owned, CAP, features)  29.1 us
    dot_general x1, matrix products, expert_block(): jnp.einsum('sekd,efd->sekf', arrived, up_weight, preferred_element_type=j...  27.1 us
    convert_element_type x1, local copies, waits for them, and re-layouts, expert_block(): return produced.astype(jnp.bfloat16)  24.1 us
    reshape x1, local copies, waits for them, and re-layouts, on_device(): results = returned.reshape(experts * CAP, features)  16.5 us
  transfers between devices with their start and end apart: 1, of which 0 were waited for; matrix products, arithmetic and copies ran while one was open for 0% of the time, Pallas kernels for 0%

profile of v1, /device:TPU:0, one launch (start us, length us, event | category | flops | bytes accessed | tf_op | source)
XLA Modules:
  0.0 721.3 jit_solution(1897470006476194372)
XLA Ops:
  0.6 0.8 copy.24
  1.4 0.1 eq.29
  1.5 0.1 eq.25
  1.6 0.7 broadcast_multiply_fusion
  2.3 0.1 copy.26
  2.4 0.2 fusion.22
  2.7 0.1 copy.27
  2.8 0.1 copy.23
  2.9 0.1 mul.34
  3.0 0.4 convert_reduce_fusion
  3.4 4.3 scatter_custom_fusion
  7.7 1.1 concatenate.3
  8.8 10.9 %gather_fusion = bf16[2560,2048]{1,0:T(8,128)(2,1)} fusion(bf16[129,2048]{1,0:T(8,128)(2,1)S(1)} %concatenate.3, s32[3072]{0:T(1024)S(1)} %pad_clamp_fusion), kind=kCustom, calls=%fused_computation | custom fusion | bytes 20981760 | tf_op jit(solution)/shard_map/gather | solution.py:34
  19.7 16.4 %reshape.69 = bf16[32,4,20,2048]{3,2,1,0:T(8,128)(2,1)} reshape(bf16[2560,2048]{1,0:T(8,128)(2,1)} %gather_fusion) | data formatting | bytes 20971520 | tf_op jit(solution)/shard_map/reshape | solution.py:34
  36.1 12.8 %copy.28 = bf16[32,4,20,2048]{3,1,2,0:T(4,128)(2,1)S(1)} copy(bf16[32,4,20,2048]{3,2,1,0:T(8,128)(2,1)} %reshape.69) | data formatting | bytes 20971520 | tf_op jit(solution)/shard_map/reshape | solution.py:34
  48.9 237.0 %all_to_all.10 = bf16[32,4,20,2048]{3,1,2,0:T(4,128)(2,1)} all-to-all(bf16[32,4,20,2048]{3,1,2,0:T(4,128)(2,1)S(1)} %copy.28), channel_id=1, replica_groups=mesh['dp'=4,'expert'=8] {'dp','expert'}, dimensions={0} | all-to-all | bytes 20971520 | tf_op jit(solution)/shard_map/all_to_all | solution.py:42
  285.8 27.1 %fusion.2 = f32[4,32,20,768]{3,1,2,0:T(8,128)} fusion(bf16[4,768,2048]{2,1,0:T(8,128)(2,1)} %param.10, bf16[32,4,20,2048]{3,1,2,0:T(4,128)(2,1)} %all_to_all.10), kind=kOutput, calls=%fused_computation.5 | convolution fusion | flops 8053063680 | bytes 30932992 | tf_op jit(solution)/shard_map/sekd,efd->sekf/dot_general | solution.py:13
  313.0 32.5 %fusion.8 = bf16[32,4,20,768]{3,0,2,1:T(8,128)(2,1)} fusion(f32[4,32,20,768]{3,1,2,0:T(8,128)} %fusion.2, bf16[4,768,2048]{2,1,0:T(8,128)(2,1)} %param.9, bf16[32,4,20,2048]{3,1,2,0:T(4,128)(2,1)} %all_to_all.10), kind=kOutput, calls=%fused_computation.13 | convolution fusion | flops 8064860160 | bytes 34865152 | tf_op jit(solution)/shard_map/sekd,efd->sekf/dot_general | solution.py:10
  345.4 13.7 %convert_bitcast_fusion = bf16[32,4,20,2048]{3,0,2,1:T(8,128)(2,1)S(1)} fusion(bf16[32,4,20,768]{3,0,2,1:T(8,128)(2,1)} %fusion.8, bf16[4,768,2048]{2,1,0:T(8,128)(2,1)} %param.11), kind=kOutput, calls=%fused_computation.9 | convolution fusion | flops 8058306560 | bytes 27000832 | tf_op jit(solution)/shard_map/sekf,efd->sekd/dot_general | solution.py:15
  359.1 24.1 %copy.31 = bf16[32,4,20,2048]{3,1,2,0:T(4,128)(2,1)} copy(bf16[32,4,20,2048]{3,0,2,1:T(8,128)(2,1)S(1)} %convert_bitcast_fusion) | data formatting | bytes 20971520 | tf_op jit(solution)/shard_map/convert_element_type | solution.py:16
  383.2 0.0 copy-start
  383.2 3.9 all-to-all-start.1
  387.1 0.0 copy-done
  387.1 0.1 copy.36
  387.3 284.0 %all-gather.1 = f32[32,1,128]{2,1,0:T(1,128)S(1)} all-gather(f32[1,1,128]{2,1,0:T(1,128)S(1)} %convert_bitcast_fusion.1), channel_id=2, replica_groups=mesh['dp'=4,'expert'=8] {'dp','expert'}, dimensions={0}, use_global_device_ids=true | all-gather | bytes 16896 | tf_op jit(solution)/shard_map/all_gather | solution.py:37
  671.3 0.1 reduce_sum.42
  671.4 0.5 broadcast_multiply_fusion.1
  671.9 0.0 all-to-all-done.1
  671.9 14.3 %copy.32 = bf16[32,4,20,2048]{3,2,1,0:T(8,128)(2,1)} copy(bf16[32,4,20,2048]{3,1,2,0:T(4,128)(2,1)} %all-to-all-done.1) | data formatting | bytes 20971520 | tf_op jit(solution)/shard_map/all_to_all | solution.py:47
  686.2 16.5 %reshape.70 = bf16[2560,2048]{1,0:T(8,128)(2,1)} reshape(bf16[32,4,20,2048]{3,2,1,0:T(8,128)(2,1)} %copy.32) | data formatting | bytes 20971520 | tf_op jit(solution)/shard_map/reshape | solution.py:48
  702.7 14.2 %gather_fusion.1 = bf16[1024,2048]{1,0:T(8,128)(2,1)} fusion(bf16[2560,2048]{1,0:T(8,128)(2,1)} %reshape.70, s32[1024]{0:T(1024)S(1)} %broadcast_clamp_fusion), kind=kCustom, calls=%fused_computation.1 | custom fusion | bytes 8392704 | tf_op jit(solution)/shard_map/gather | solution.py:49
  716.8 3.4 fusion.18
  720.3 1.1 copy.45
  (12 shorter events, 0.1 us)
Async XLA Ops:
  383.2 3.9 copy-start
  383.2 288.7 %all-to-all-start.1 = ((bf16[32,4,20,2048]{3,1,2,0:T(4,128)(2,1)}), bf16[32,4,20,2048]{3,1,2,0:T(4,128)(2,1)}, u32[]{:S(2)}, u32[]{:S(2)}) async-start(bf16[32,4,20,2048]{3,1,2,0:T(4,128)(2,1)} %copy.31), calls=%async_computation.1 | async-start | bytes 20971520 | tf_op jit(solution)/shard_map/all_to_all | solution.py:47
